TPU v7x, 32 devices: a whole 2x2x4 slice. The times are simulated.
32 devices in a mesh: rep: 16 (over z, x, core), shard: 2 (over y).
Axes of the slice: x: 2, y: 2, z: 4, core: 2. Of those that a mesh axis runs over, the one named last changes fastest.
Arguments:
- tokens: bfloat16 [32, 197, 512], P(('rep', 'shard')), may hold values from -6 to 6
- norm_one: bfloat16 [512], P('shard'), may hold values from 0.099609375 to 1.8984375
- w_qkv: bfloat16 [512, 1536], P('shard'), may hold values from -0.25 to 0.25
- w_attn: bfloat16 [512, 512], P('shard'), may hold values from -1 to 1
- norm_two: bfloat16 [512], P('shard'), may hold values from 0.099609375 to 1.8984375
- w_gate: bfloat16 [512, 4], P('shard'), may hold values from -0.1875 to 0.1875
- w_expin: bfloat16 [4, 512, 2048], P(None, 'shard'), may hold values from -0.25 to 0.25
- w_expout: bfloat16 [4, 2048, 512], P(None, 'shard'), may hold values from -0.125 to 0.125
- routes: int32 [32, 197, 2], P(('rep', 'shard')), may hold values from 0 to 3, all different within a row
- cotangent: bfloat16 [32, 197, 512], P(('rep', 'shard')), may hold values from -6 to 6
Outputs:
- output: bfloat16 [32, 197, 512], P(('rep', 'shard'))
- grad_tokens: bfloat16 [32, 197, 512], P(('rep', 'shard'))
- grad_norm_one: float32 [512], P('shard')
- grad_qkv: float32 [512, 1536], P('shard')
- grad_attn: float32 [512, 512], P('shard')
- grad_norm_two: float32 [512], P('shard')
- grad_gate: float32 [512, 4], P('shard')
- grad_expin: float32 [4, 512, 2048], P(None, 'shard')
- grad_expout: float32 [4, 2048, 512], P(None, 'shard')
Inputs may be any that keep to these rules, and one draw needn't show every extreme that they name: `routes`: each token names two different experts; every expert is named by some token.
All inputs are finite; a program needn't handle non-finite values.
Results may differ from a plain program's by a relative error of at most 0.024.
Values may be sent and summed in bfloat16 or wider, within the bound.
A program may use at most 192 MiB of HBM per device.

v0:
```python
from functools import partial
import jax
import jax.numpy as jnp
from jax import lax
from jax.sharding import PartitionSpec as P

HEADS = 8
HEAD_DIM = 64
norm_eps = 1e-06
highest = lax.Precision.HIGHEST
fdt = jnp.float32
bdt = jnp.bfloat16


def layer_norm(inputs, gain_vec):
    centre = inputs - jnp.mean(inputs, axis=-1, keepdims=True)
    variance = jnp.mean(centre * centre, axis=-1, keepdims=True)
    inv_root = lax.rsqrt(variance + norm_eps)
    normed = centre * inv_root
    return (normed * gain_vec, normed, inv_root)


def norm_back(grad_out, normed, inv_root, gain_vec):
    scaled = grad_out * gain_vec
    back = inv_root * (
        scaled
        - jnp.mean(scaled, axis=-1, keepdims=True)
        - normed * jnp.mean(scaled * normed, axis=-1, keepdims=True)
    )
    return (back, jnp.sum(grad_out * normed, axis=0))


def forward(weights, tokens, routes, kept_total):
    norm_one, w_qkv, w_attn, norm_two, w_gate, w_expin, w_expout = weights
    images, seq_len, model_width = tokens.shape
    tok_rows = images * seq_len
    resid = tokens.reshape(tok_rows, model_width).astype(fdt)
    hidden_one, normed_one, root_one = layer_norm(resid, norm_one.astype(fdt))
    hidden_one_low = hidden_one.astype(bdt)
    proj = jnp.dot(hidden_one_low, w_qkv, preferred_element_type=fdt).astype(bdt)
    proj = proj.reshape(images, seq_len, 3, HEADS, HEAD_DIM)
    queries = proj[:, :, 0]
    key_rows = proj[:, :, 1]
    val_rows = proj[:, :, 2]
    score_scale = HEAD_DIM ** (-0.5)
    scores = (
        jnp.einsum("ishd,ithd->ihst", queries, key_rows, preferred_element_type=fdt) * score_scale
    )
    if kept_total is None:
        log_total = jax.nn.logsumexp(scores, axis=-1, keepdims=True)
    else:
        log_total = kept_total
    soft_probs = jnp.exp(scores - log_total)
    probs_low = soft_probs.astype(bdt)
    attn_rows = jnp.einsum("ihst,ithd->ishd", probs_low, val_rows, preferred_element_type=fdt)
    attn_rows = attn_rows.reshape(tok_rows, model_width).astype(bdt)
    mixed = resid + jnp.dot(attn_rows, w_attn, preferred_element_type=fdt)
    gate_gain = norm_two.astype(fdt)
    hidden_two, normed_two, root_two = layer_norm(mixed, gate_gain)
    router = w_gate.astype(fdt)
    logits = jnp.dot(hidden_two, router, precision=highest)
    expert_count = router.shape[1]
    choose = (
        routes.reshape(tok_rows, 2)[:, :, None] == jnp.arange(expert_count)[None, None, :]
    ).astype(fdt)
    picked = jnp.sum(choose * logits[:, None, :], axis=-1)
    gates = jax.nn.softmax(picked, axis=-1)
    weight_map = jnp.sum(gates[:, :, None] * choose, axis=1)
    hidden_two_low = hidden_two.astype(bdt)
    expert_inner = jnp.einsum("td,edf->etf", hidden_two_low, w_expin, preferred_element_type=fdt)
    hidden_act = jax.nn.gelu(expert_inner, approximate=False).astype(bdt)
    outer = jnp.einsum("etf,efd->etd", hidden_act, w_expout, preferred_element_type=fdt)
    combined = mixed + jnp.sum(weight_map.T[:, :, None] * outer, axis=0)
    return {
        "combined": combined,
        "log_total": log_total,
        "resid": resid,
        "normed_one": normed_one,
        "root_one": root_one,
        "hidden_one_low": hidden_one_low,
        "queries": queries,
        "key_rows": key_rows,
        "val_rows": val_rows,
        "soft_probs": soft_probs,
        "probs_low": probs_low,
        "attn_rows": attn_rows,
        "normed_two": normed_two,
        "root_two": root_two,
        "hidden_two": hidden_two,
        "hidden_two_low": hidden_two_low,
        "choose": choose,
        "gates": gates,
        "weight_map": weight_map,
        "expert_inner": expert_inner,
        "hidden_act": hidden_act,
        "outer": outer,
    }


def on_device(
    tokens, norm_one, w_qkv, w_attn, norm_two, w_gate, w_expin, w_expout, routes, cotangent
):
    images, seq_len, model_width = tokens.shape
    tok_rows = images * seq_len
    whole = (
        lax.all_gather(norm_one, "shard", axis=0, tiled=True),
        lax.all_gather(w_qkv, "shard", axis=0, tiled=True),
        lax.all_gather(w_attn, "shard", axis=0, tiled=True),
        lax.all_gather(norm_two, "shard", axis=0, tiled=True),
        lax.all_gather(w_gate, "shard", axis=0, tiled=True),
        lax.all_gather(w_expin, "shard", axis=1, tiled=True),
        lax.all_gather(w_expout, "shard", axis=1, tiled=True),
    )
    first = forward(whole, tokens, routes, None)
    output = first["combined"].reshape(images, seq_len, model_width).astype(bdt)
    again = (
        lax.all_gather(norm_one, "shard", axis=0, tiled=True),
        lax.all_gather(w_qkv, "shard", axis=0, tiled=True),
        lax.all_gather(w_attn, "shard", axis=0, tiled=True),
        lax.all_gather(norm_two, "shard", axis=0, tiled=True),
        lax.all_gather(w_gate, "shard", axis=0, tiled=True),
        lax.all_gather(w_expin, "shard", axis=1, tiled=True),
        lax.all_gather(w_expout, "shard", axis=1, tiled=True),
    )
    parts = forward(again, tokens, routes, first["log_total"])
    g_one, m_qkv, m_attn, g_two, m_gate, m_expin, m_expout = again
    gain_one = g_one.astype(fdt)
    gain_two = g_two.astype(fdt)
    router = m_gate.astype(fdt)
    dout = cotangent.reshape(tok_rows, model_width).astype(fdt)
    dweight = jnp.sum(dout[None, :, :] * parts["outer"], axis=-1).T
    dout_exp = (parts["weight_map"].T[:, :, None] * dout[None, :, :]).astype(bdt)
    grad_expout = jnp.einsum(
        "etf,etd->efd", parts["hidden_act"], dout_exp, preferred_element_type=fdt
    )
    dhidden = jnp.einsum("etd,efd->etf", dout_exp, m_expout, preferred_element_type=fdt)
    gelu_exact = partial(jax.nn.gelu, approximate=False)
    _, gelu_pull = jax.vjp(gelu_exact, parts["expert_inner"])
    dinner = gelu_pull(dhidden)[0].astype(bdt)
    grad_expin = jnp.einsum(
        "td,etf->edf", parts["hidden_two_low"], dinner, preferred_element_type=fdt
    )
    dhidden_two = jnp.einsum("etf,edf->td", dinner, m_expin, preferred_element_type=fdt)
    choose = parts["choose"]
    gates = parts["gates"]
    dpicked = jnp.sum(choose * dweight[:, None, :], axis=-1)
    gate_dot = jnp.sum(gates * dpicked, axis=-1, keepdims=True)
    dpair = gates * (dpicked - gate_dot)
    dlogits = jnp.sum(dpair[:, :, None] * choose, axis=1)
    grad_gate = jnp.dot(parts["hidden_two"].T, dlogits, precision=highest)
    dhidden_two = dhidden_two + jnp.dot(dlogits, router.T, precision=highest)
    dmixed_norm, grad_norm_two = norm_back(
        dhidden_two, parts["normed_two"], parts["root_two"], gain_two
    )
    dmixed = dout + dmixed_norm
    dmixed_low = dmixed.astype(bdt)
    grad_attn = jnp.dot(parts["attn_rows"].T, dmixed_low, preferred_element_type=fdt)
    dattn = jnp.dot(dmixed_low, m_attn.T, preferred_element_type=fdt).astype(bdt)
    dattn = dattn.reshape(images, seq_len, HEADS, HEAD_DIM)
    dprobs = jnp.einsum("ishd,ithd->ihst", dattn, parts["val_rows"], preferred_element_type=fdt)
    dvalues = jnp.einsum("ihst,ishd->ithd", parts["probs_low"], dattn, preferred_element_type=fdt)
    soft_probs = parts["soft_probs"]
    row_delta = jnp.sum(dprobs * soft_probs, axis=-1, keepdims=True)
    dscores = (soft_probs * (dprobs - row_delta)).astype(bdt)
    score_scale = HEAD_DIM ** (-0.5)
    dqueries = (
        jnp.einsum("ihst,ithd->ishd", dscores, parts["key_rows"], preferred_element_type=fdt)
        * score_scale
    )
    dkeys = (
        jnp.einsum("ihst,ishd->ithd", dscores, parts["queries"], preferred_element_type=fdt)
        * score_scale
    )
    dproj = (
        jnp.stack([dqueries, dkeys, dvalues], axis=2).reshape(tok_rows, 3 * model_width).astype(bdt)
    )
    grad_qkv = jnp.dot(parts["hidden_one_low"].T, dproj, preferred_element_type=fdt)
    dhidden_one = jnp.dot(dproj, m_qkv.T, preferred_element_type=fdt)
    dresid_norm, grad_norm_one = norm_back(
        dhidden_one, parts["normed_one"], parts["root_one"], gain_one
    )
    grad_tokens = (dmixed + dresid_norm).reshape(images, seq_len, model_width).astype(bdt)
    owned = (
        lax.psum_scatter(
            grad_norm_one.astype(jnp.bfloat16), "shard", scatter_dimension=0, tiled=True
        ).astype(jnp.float32),
        lax.psum_scatter(
            grad_qkv.astype(jnp.bfloat16), "shard", scatter_dimension=0, tiled=True
        ).astype(jnp.float32),
        lax.psum_scatter(
            grad_attn.astype(jnp.bfloat16), "shard", scatter_dimension=0, tiled=True
        ).astype(jnp.float32),
        lax.psum_scatter(
            grad_norm_two.astype(jnp.bfloat16), "shard", scatter_dimension=0, tiled=True
        ).astype(jnp.float32),
        lax.psum_scatter(
            grad_gate.astype(jnp.bfloat16), "shard", scatter_dimension=0, tiled=True
        ).astype(jnp.float32),
        lax.psum_scatter(
            grad_expin.astype(jnp.bfloat16), "shard", scatter_dimension=1, tiled=True
        ).astype(jnp.float32),
        lax.psum_scatter(
            grad_expout.astype(jnp.bfloat16), "shard", scatter_dimension=1, tiled=True
        ).astype(jnp.float32),
    )
    summed = (
        lax.psum(owned[0].astype(jnp.bfloat16), "rep").astype(jnp.float32),
        lax.psum(owned[1].astype(jnp.bfloat16), "rep").astype(jnp.float32),
        lax.psum(owned[2].astype(jnp.bfloat16), "rep").astype(jnp.float32),
        lax.psum(owned[3].astype(jnp.bfloat16), "rep").astype(jnp.float32),
        lax.psum(owned[4].astype(jnp.bfloat16), "rep").astype(jnp.float32),
        lax.psum(owned[5].astype(jnp.bfloat16), "rep").astype(jnp.float32),
        lax.psum(owned[6].astype(jnp.bfloat16), "rep").astype(jnp.float32),
    )
    return (
        output,
        grad_tokens,
        summed[0],
        summed[1],
        summed[2],
        summed[3],
        summed[4],
        summed[5],
        summed[6],
    )


def solution(mesh):
    placed = (
        P(("rep", "shard"), None, None),
        P("shard"),
        P("shard", None),
        P("shard", None),
        P("shard"),
        P("shard", None),
        P(None, "shard", None),
        P(None, "shard", None),
        P(("rep", "shard"), None, None),
        P(("rep", "shard"), None, None),
    )
    return jax.shard_map(
        on_device,
        mesh=mesh,
        in_specs=placed,
        out_specs=(
            P(("rep", "shard"), None, None),
            P(("rep", "shard"), None, None),
            P("shard"),
            P("shard", None),
            P("shard", None),
            P("shard"),
            P("shard", None),
            P(None, "shard", None),
            P(None, "shard", None),
        ),
        check_vma=False,
    )
```

profile of v0, /device:TPU:0, one launch (start us, length us, event | category | flops | bytes accessed | tf_op | source)
XLA Modules:
  0.0 764.5 jit_solution(5038029769242780368)
XLA Ops:
  9.7 5.2 all-gather
  14.8 4.2 all-gather.1
  19.1 4.3 all_gather.32
  23.7 14.0 %all_gather.30 = bf16[512,512]{1,0:T(8,128)(2,1)} all-gather(bf16[256,512]{1,0:T(8,128)(2,1)S(1)} %copy-done.11), channel_id=1, replica_groups=mesh['rep'=16,'shard'=2] {'shard'}, dimensions={0}, use_global_device_ids=true | all-gather | bytes 786432 | tf_op jit(solution)/shard_map/all_gather | solution.py:108
  38.5 6.7 all-gather.6.cloned.1.call-done
  51.5 99.3 %all-gather.8.cloned.1.call-done = bf16[4,512,2048]{2,1,0:T(8,128)(2,1)} async-done(((bf16[4,256,2048]{2,1,0:T(8,128)(2,1)}), bf16[4,512,2048]{2,1,0:T(8,128)(2,1)}) %all-gather.8.cloned.1.call-update) | async-done | bytes 8388624 | tf_op jit(solution)/shard_map/all_gather | solution.py:111
  150.8 18.8 %fusion.2 = (bf16[4,197,2048]{2,1,0:T(8,128)(2,1)}, f32[4,197,2048]{2,1,0:T(8,128)}, f32[197,4,2048]{2,0,1:T(8,128)}) fusion(bf16[4,512,2048]{2,1,0:T(8,128)(2,1)} %all-gather.8.cloned.1.call-done, f32[512]{0:T(512)S(1)} %bitcast.219, f32[197]{0:T(256)S(1)} %add_rsqrt_fusion, f32[197,512]{1,0:T(8,128)S(1)} %get-tuple-element.69, ...), kind=kOutput, calls=%fused_computation.10 | convolution fusion | flops 1757857792 | bytes 24933928 | tf_op jit(solution)/shard_map/td,edf->etf/dot_general | solution.py:70
  169.6 86.8 %all-gather.10.cloned.1.call-done = bf16[4,2048,512]{2,1,0:T(8,128)(2,1)} async-done(((bf16[4,1024,512]{2,1,0:T(8,128)(2,1)}), bf16[4,2048,512]{2,1,0:T(8,128)(2,1)}) %all-gather.10.cloned.1.call-update) | async-done | bytes 8388624 | tf_op jit(solution)/shard_map/all_gather | solution.py:112
  256.4 6.5 multiply_reduce_fusion.1
  263.0 11.2 %fusion.8 = bf16[4,197,2048]{2,1,0:T(8,128)(2,1)S(1)} fusion(f32[4,197,2048]{2,1,0:T(8,128)} %get-tuple-element.63, f32[197,4,2048]{2,0,1:T(8,128)} %get-tuple-element.70, bf16[4,2048,512]{2,1,0:T(8,128)(2,1)} %all-gather.10.cloned.1.call-done, f32[197,512]{1,0:T(8,128)S(1)} %copy-done.6, f32[4,197]{1,0:T(4,128)S(1)} %bitcast.233), kind=kOutput, calls=%fused_computation.16 | convolution fusion | flops 1675956224 | bytes 24933456 | tf_op jit(solution)/shard_map/etd,efd->etf/dot_general | solution.py:136
  274.3 7.4 convolution_bitcast_fusion.1
  287.0 2.6 multiply_reduce_fusion
  295.0 8.1 %convert_bitcast_fusion = bf16[4,512,2048]{1,2,0:T(8,128)(2,1)} fusion(bf16[4,197,2048]{2,1,0:T(8,128)(2,1)} %copy-done.1, f32[512]{0:T(512)S(1)} %bitcast.222, f32[197,512]{1,0:T(8,128)S(1)} %get-tuple-element.69, f32[197]{0:T(256)S(1)} %add_rsqrt_fusion, f32[197]{0:T(256)S(1)} %broadcast_multiply_fusion.4), kind=kOutput, calls=%fused_computation.1 | convolution fusion | flops 1657153536 | bytes 12023336 | tf_op jit(solution)/shard_map/td,etf->edf/dot_general | solution.py:140
  304.1 7.9 %convolution_convert_fusion = bf16[4,2048,512]{2,1,0:T(8,128)(2,1)} fusion(bf16[4,197,2048]{2,1,0:T(8,128)(2,1)} %get-tuple-element.62, f32[197,512]{1,0:T(8,128)S(1)} %copy-done.7, f32[4,197]{1,0:T(4,128)S(1)} %bitcast.234), kind=kOutput, calls=%fused_computation.30 | convolution fusion | flops 1657556992 | bytes 12022864 | tf_op jit(solution)/shard_map/etf,etd->efd/dot_general | solution.py:133
  313.4 19.7 %reduce-scatter.8.cloned.1.call-done = bf16[256,1536]{1,0:T(8,128)(2,1)} async-done(((bf16[512,1536]{1,0:T(8,128)(2,1)}), bf16[256,1536]{1,0:T(8,128)(2,1)}) %reduce-scatter.8.cloned.1.call-update) | async-done | bytes 786448 | tf_op jit(solution)/shard_map/reduce_scatter | solution.py:187
  333.2 102.0 %reduce-scatter.12.cloned.1.call-done = bf16[4,256,2048]{1,2,0:T(8,128)(2,1)} async-done(((bf16[4,512,2048]{1,2,0:T(8,128)(2,1)}), bf16[4,256,2048]{1,2,0:T(8,128)(2,1)}) %reduce-scatter.12.cloned.1.call-update) | async-done | bytes 4194320 | tf_op jit(solution)/shard_map/reduce_scatter | solution.py:199
  435.2 102.2 %reduce-scatter.14.cloned.1.call-done = bf16[4,1024,512]{2,1,0:T(8,128)(2,1)} async-done(((bf16[4,2048,512]{2,1,0:T(8,128)(2,1)}), bf16[4,1024,512]{2,1,0:T(8,128)(2,1)}) %reduce-scatter.14.cloned.1.call-update) | async-done | bytes 4194320 | tf_op jit(solution)/shard_map/reduce_scatter | solution.py:202
  539.5 4.9 all-reduce.4
  545.5 4.4 reduce-scatter.16.cloned.1.call-done
  550.9 34.5 %all-reduce.2 = (bf16[256]{0:T(256)(128)(2,1)S(1)}, bf16[256]{0:T(256)(128)(2,1)S(1)}, bf16[256,4]{0,1:T(4,128)(2,1)S(1)}) all-reduce(bf16[256]{0:T(256)(128)(2,1)S(1)} %dynamic-slice.1, bf16[256]{0:T(256)(128)(2,1)S(1)} %dynamic-slice.3, bf16[256,4]{0,1:T(4,128)(2,1)S(1)} %copy.62), channel_id=1, replica_groups=mesh['rep'=16,'shard'=2] {'rep'}, use_global_device_ids=true, to_apply=%region_22.0 | all-reduce | flops 1536 | bytes 6144 | tf_op jit(solution)/shard_map/psum | solution.py:207
  587.1 153.0 %all-reduce.7.cloned.1.call-done = (bf16[4,256,2048]{1,2,0:T(8,128)(2,1)}, bf16[256,1536]{1,0:T(8,128)(2,1)}, bf16[256,512]{1,0:T(8,128)(2,1)}, bf16[4,1024,512]{2,1,0:T(8,128)(2,1)}) async-done(((bf16[4,256,2048]{1,2,0:T(8,128)(2,1)}, bf16[256,1536]{1,0:T(8,128)(2,1)}, bf16[256,512]{1,0:T(8,128)(2,1)}, bf16[4,1024,512]{2,1,0:T(8,128)(2,1)}), (bf16[4,256,2048]{1,2,0:T(8,128)(2,1)}, ...) | async-done | bytes 9437200 | tf_op jit(solution)/shard_map/psum | solution.py:212
  740.0 2.5 convert_element_type.206
  744.3 6.9 copy.56
  751.2 6.8 convert_element_type.217
  (109 shorter events, 29.7 us)
Async XLA Ops:
  7.2 2.3 copy-start
  7.2 2.4 copy-start.14
  7.2 7.6 copy-start.15
  7.2 11.9 %copy-start.13 = (bf16[256,4]{0,1:T(4,128)(2,1)S(1)}, bf16[256,4]{0,1:T(4,128)(2,1)}, u32[]{:S(2)}) copy-start(bf16[256,4]{0,1:T(4,128)(2,1)} %param.15) | copy-start | bytes 6148
  7.2 16.4 %copy-start.11 = (bf16[256,512]{1,0:T(8,128)(2,1)S(1)}, bf16[256,512]{1,0:T(8,128)(2,1)}, u32[]{:S(2)}) copy-start(bf16[256,512]{1,0:T(8,128)(2,1)} %param.13) | copy-start | bytes 786436
  7.2 30.5 %copy-start.9 = (bf16[1,197,512]{2,1,0:T(8,128)(2,1)S(1)}, bf16[1,197,512]{2,1,0:T(8,128)(2,1)}, u32[]{:S(2)}) copy-start(bf16[1,197,512]{2,1,0:T(8,128)(2,1)} %param.19) | copy-start | bytes 605188
  7.2 38.0 %all-gather.6.cloned.1.call-start = ((), (), s32[]{:S(2)}) async-start(), calls=%async_computation.5 | async-start | bytes 2359296 | tf_op jit(solution)/shard_map/all_gather | solution.py:107
  8.0 142.8 %all-gather.8.cloned.1.call-start = ((), (), s32[]{:S(2)}) async-start(), calls=%async_computation.6 | async-start | bytes 12582912 | tf_op jit(solution)/shard_map/all_gather | solution.py:111
  8.7 247.7 %all-gather.10.cloned.1.call-start = ((), (), s32[]{:S(2)}) async-start(), calls=%async_computation.7 | async-start | bytes 12582912 | tf_op jit(solution)/shard_map/all_gather | solution.py:112
  9.5 304.0 %reduce-scatter.10.cloned.1.call-start = ((), (), s32[]{:S(2)}) async-start(), calls=%async_computation.9 | async-start | bytes 786432 | tf_op jit(solution)/shard_map/reduce_scatter | solution.py:190
  23.7 27.7 %copy-start.12 = (s32[1,197,2]{1,2,0:T(2,128)S(1)}, s32[1,197,2]{1,2,0:T(2,128)}, u32[]{:S(2)}) copy-start(s32[1,197,2]{1,2,0:T(2,128)} %param.18) | copy-start | bytes 4732
  51.5 204.9 %copy-start.6 = (f32[197,512]{1,0:T(8,128)S(1)}, f32[197,512]{1,0:T(8,128)}, u32[]{:S(2)}) copy-start(f32[197,512]{1,0:T(8,128)} %bitcast_convert_fusion) | copy-start | bytes 1210372
  274.2 7.5 copy-start.1
  274.2 8.1 %copy-start.10 = (bf16[1,197,512]{2,1,0:T(8,128)(2,1)S(1)}, bf16[1,197,512]{2,1,0:T(8,128)(2,1)}, u32[]{:S(2)}) copy-start(bf16[1,197,512]{2,1,0:T(8,128)(2,1)} %param.19) | copy-start | bytes 605188
  274.2 8.9 %copy-start.2 = (bf16[512,512]{1,0:T(8,128)(2,1)S(1)}, bf16[512,512]{1,0:T(8,128)(2,1)}, u32[]{:S(2)}) copy-start(bf16[512,512]{1,0:T(8,128)(2,1)} %all_gather.30) | copy-start | bytes 1572868
  274.2 9.9 %copy-start.4 = (bf16[8,64,197]{2,1,0:T(8,128)(2,1)S(1)}, bf16[8,64,197]{2,1,0:T(8,128)(2,1)}, u32[]{:S(2)}) copy-start(bf16[8,64,197]{2,1,0:T(8,128)(2,1)} %copy-done.3) | copy-start | bytes 605188
  289.6 43.6 %reduce-scatter.8.cloned.1.call-start = ((), (), s32[]{:S(2)}) async-start(), calls=%async_computation.8 | async-start | bytes 2359296 | tf_op jit(solution)/shard_map/reduce_scatter | solution.py:187
  289.8 2.6 copy-start.5
  294.9 140.2 %reduce-scatter.12.cloned.1.call-start = ((), (), s32[]{:S(2)}) async-start(), calls=%async_computation.10 | async-start | bytes 12582912 | tf_op jit(solution)/shard_map/reduce_scatter | solution.py:199
  303.1 234.3 %reduce-scatter.14.cloned.1.call-start = ((), (), s32[]{:S(2)}) async-start(), calls=%async_computation.11 | async-start | bytes 12582912 | tf_op jit(solution)/shard_map/reduce_scatter | solution.py:202
  312.0 225.4 %copy-start.16 = (u32[32]{0:T(128)S(1)}, u32[32]{0:T(128)}, u32[]{:S(2)}) copy-start(u32[32]{0:T(128)} %constant.92) | copy-start | bytes 388
  312.0 226.7 %copy-start.8 = (bf16[512,1536]{1,0:T(8,128)(2,1)S(1)}, bf16[512,1536]{1,0:T(8,128)(2,1)}, u32[]{:S(2)}) copy-start(bf16[512,1536]{1,0:T(8,128)(2,1)} %all-gather.6.cloned.1.call-done) | copy-start | bytes 4718596
  312.0 237.9 %reduce-scatter.16.cloned.1.call-start = ((), (), s32[]{:S(2)}) async-start(), calls=%async_computation.12 | async-start | bytes 196608
  313.3 426.7 %all-reduce.7.cloned.1.call-start = ((), (), s32[]{:S(2)}) async-start(), calls=%async_computation.13 | async-start | bytes 18874368 | tf_op jit(solution)/shard_map/psum | solution.py:212
  (2 other events, 1.7 us)
Sparse Core Ops, SparseCore 0:
  9.6 35.5 all-gather.5
  46.7 103.9 all-gather.7
  152.3 103.9 all-gather.9
  289.7 14.5 reduce-scatter.9
  307.0 26.0 reduce-scatter.7
  335.9 99.2 reduce-scatter.11
  438.1 99.2 reduce-scatter.13
  539.6 10.2 reduce-scatter.15
  553.9 186.0 all-reduce.6
where the time goes:
time: 765 us; the launch traced here: 764 us
  waiting for transfers between devices  576 us (75%)
  matrix products  74.1 us (10%)
  blocking collectives  67.2 us (9%)
  other arithmetic  18.4 us (2%)
  between operations  14.8 us (2%)
  local copies, waits for them, and re-layouts  13.1 us (2%)
    psum x1, waiting for transfers between devices, on_device(): lax.psum(owned[5].astype(jnp.bfloat16), 'rep').astype(jnp.float32)  153 us
    reduce_scatter x1, waiting for transfers between devices, on_device(): lax.psum_scatter(grad_expout.astype(jnp.bfloat16), 'shard', scatter_dimen...  102 us
    reduce_scatter x1, waiting for transfers between devices, on_device(): lax.psum_scatter(grad_expin.astype(jnp.bfloat16), 'shard', scatter_dimens...  102 us
    all_gather x1, waiting for transfers between devices, on_device(): lax.all_gather(w_expin, 'shard', axis=1, tiled=True)  99.3 us
    all_gather x1, waiting for transfers between devices, on_device(): lax.all_gather(w_expout, 'shard', axis=1, tiled=True)  86.8 us
    psum x1, blocking collectives, on_device(): lax.psum(owned[0].astype(jnp.bfloat16), 'rep').astype(jnp.float32)  34.5 us
    reduce_scatter x1, waiting for transfers between devices, on_device(): lax.psum_scatter(grad_qkv.astype(jnp.bfloat16), 'shard', scatter_dimensio...  19.7 us
    dot_general x1, matrix products, forward(): jnp.einsum('td,edf->etf', hidden_two_low, w_expin, preferred_element_type...  18.8 us
  transfers between devices with their start and end apart: 9, of which 8 were waited for; matrix products, arithmetic and copies ran while one was open for 7% of the time, Pallas kernels for 0%

commit v1 on v0

--- a/solution.py
+++ b/solution.py
@@ -209,7 +209,7 @@
         lax.psum(owned[2].astype(jnp.bfloat16), "rep").astype(jnp.float32),
         lax.psum(owned[3].astype(jnp.bfloat16), "rep").astype(jnp.float32),
         lax.psum(owned[4].astype(jnp.bfloat16), "rep").astype(jnp.float32),
-        lax.psum(owned[5].astype(jnp.bfloat16), "rep").astype(jnp.float32),
+        jnp.sum(lax.all_gather(owned[5].astype(jnp.bfloat16), "rep"), axis=0).astype(jnp.float32),
         lax.psum(owned[6].astype(jnp.bfloat16), "rep").astype(jnp.float32),
     )
     return (

time: 765 us -> 1050 us (1.37)
  waiting for transfers between devices: 576 us -> 826 us
  other arithmetic: 18.4 us -> 42.8 us
  local copies, waits for them, and re-layouts: 13.1 us -> 24.5 us
    all_gather x0 -> x1, waiting for transfers between devices: none -> 315 us  [on_device(): lax.all_gather(owned[5].astype(jnp.bfloat16), 'rep')]
    psum x1, waiting for transfers between devices: 153 us -> 91.7 us  [on_device(): lax.psum(owned[1].astype(jnp.bfloat16), 'rep').astype(jnp.float32)]
    reduce_sum x0 -> x1, other arithmetic: none -> 23.8 us  [on_device(): jnp.sum(lax.all_gather(owned[5].astype(jnp.bfloat16), 'rep'), axis=0)]
  transfers between devices with their start and end apart: 9 -> 10, of which waited for: 8 -> 8; matrix products, arithmetic and copies ran while one was open for 7% -> 7% of each run, Pallas kernels for 0% -> 0%
where the time goes in v1:
time: 1050 us
  waiting for transfers between devices  826 us (79%)
  matrix products  73.1 us (7%)
  blocking collectives  66.5 us (6%)
  other arithmetic  42.8 us (4%)
  local copies, waits for them, and re-layouts  24.5 us (2%)
  between operations  15.2 us (1%)
    all_gather x1, waiting for transfers between devices, on_device(): lax.all_gather(owned[5].astype(jnp.bfloat16), 'rep')  315 us
    reduce_scatter x1, waiting for transfers between devices, on_device(): lax.psum_scatter(grad_expin.astype(jnp.bfloat16), 'shard', scatter_dimens...  102 us
    reduce_scatter x1, waiting for transfers between devices, on_device(): lax.psum_scatter(grad_expout.astype(jnp.bfloat16), 'shard', scatter_dimen...  102 us
    all_gather x1, waiting for transfers between devices, on_device(): lax.all_gather(w_expin, 'shard', axis=1, tiled=True)  99.3 us
    psum x1, waiting for transfers between devices, on_device(): lax.psum(owned[1].astype(jnp.bfloat16), 'rep').astype(jnp.float32)  91.7 us
    all_gather x1, waiting for transfers between devices, on_device(): lax.all_gather(w_expout, 'shard', axis=1, tiled=True)  86.8 us
    psum x1, blocking collectives, on_device(): lax.psum(owned[0].astype(jnp.bfloat16), 'rep').astype(jnp.float32)  33.8 us
    reduce_sum x1, other arithmetic, on_device(): jnp.sum(lax.all_gather(owned[5].astype(jnp.bfloat16), 'rep'), axis=0)  23.8 us
  transfers between devices with their start and end apart: 10, of which 8 were waited for; matrix products, arithmetic and copies ran while one was open for 7% of the time, Pallas kernels for 0%

profile of v1, /device:TPU:0, one launch (start us, length us, event | category | flops | bytes accessed | tf_op | source)
XLA Modules:
  0.0 1049.0 jit_solution(5029005607172778200)
XLA Ops:
  9.7 5.2 all-gather.1
  19.1 4.3 all_gather.38
  23.7 14.0 %all_gather.36 = bf16[512,512]{1,0:T(8,128)(2,1)} all-gather(bf16[256,512]{1,0:T(8,128)(2,1)S(1)} %copy-done.10), channel_id=1, replica_groups=mesh['rep'=16,'shard'=2] {'shard'}, dimensions={0}, use_global_device_ids=true | all-gather | bytes 786432 | tf_op jit(solution)/shard_map/all_gather | solution.py:108
  38.5 6.7 all-gather.8.cloned.1.call-done
  51.5 99.3 %all-gather.10.cloned.1.call-done = bf16[4,512,2048]{2,1,0:T(8,128)(2,1)} async-done(((bf16[4,256,2048]{2,1,0:T(8,128)(2,1)}), bf16[4,512,2048]{2,1,0:T(8,128)(2,1)}) %all-gather.10.cloned.1.call-update) | async-done | bytes 8388624 | tf_op jit(solution)/shard_map/all_gather | solution.py:111
  150.8 18.8 %fusion.2 = (bf16[4,197,2048]{2,1,0:T(8,128)(2,1)}, f32[4,197,2048]{2,1,0:T(8,128)}, f32[197,4,2048]{2,0,1:T(8,128)}) fusion(bf16[4,512,2048]{2,1,0:T(8,128)(2,1)} %all-gather.10.cloned.1.call-done, f32[512]{0:T(512)S(1)} %bitcast.220, f32[197]{0:T(256)S(1)} %add_rsqrt_fusion, f32[197,512]{1,0:T(8,128)S(1)} %get-tuple-element.50, ...), kind=kOutput, calls=%fused_computation.10 | convolution fusion | flops 1757857792 | bytes 24933928 | tf_op jit(solution)/shard_map/td,edf->etf/dot_general | solution.py:70
  169.6 86.8 %all-gather.12.cloned.1.call-done = bf16[4,2048,512]{2,1,0:T(8,128)(2,1)} async-done(((bf16[4,1024,512]{2,1,0:T(8,128)(2,1)}), bf16[4,2048,512]{2,1,0:T(8,128)(2,1)}) %all-gather.12.cloned.1.call-update) | async-done | bytes 8388624 | tf_op jit(solution)/shard_map/all_gather | solution.py:112
  256.4 6.5 multiply_reduce_fusion.1
  263.0 11.2 %fusion.8 = bf16[4,197,2048]{2,1,0:T(8,128)(2,1)S(1)} fusion(f32[4,197,2048]{2,1,0:T(8,128)} %get-tuple-element.44, f32[197,4,2048]{2,0,1:T(8,128)} %get-tuple-element.51, bf16[4,2048,512]{2,1,0:T(8,128)(2,1)} %all-gather.12.cloned.1.call-done, f32[197,512]{1,0:T(8,128)S(1)} %copy-done.6, f32[4,197]{1,0:T(4,128)S(1)} %bitcast.234), kind=kOutput, calls=%fused_computation.16 | convolution fusion | flops 1675956224 | bytes 24933456 | tf_op jit(solution)/shard_map/etd,efd->etf/dot_general | solution.py:136
  274.3 7.4 convolution_bitcast_fusion.1
  292.5 8.0 convolution_convert_fusion
  300.6 8.1 convert_bitcast_fusion
  310.0 20.6 %reduce-scatter.8.cloned.1.call-done = bf16[256,1536]{1,0:T(8,128)(2,1)} async-done(((bf16[512,1536]{1,0:T(8,128)(2,1)}), bf16[256,1536]{1,0:T(8,128)(2,1)}) %reduce-scatter.8.cloned.1.call-update) | async-done | bytes 786448 | tf_op jit(solution)/shard_map/reduce_scatter | solution.py:187
  330.6 102.0 %reduce-scatter.14.cloned.1.call-done = bf16[4,1024,512]{2,1,0:T(8,128)(2,1)} async-done(((bf16[4,2048,512]{2,1,0:T(8,128)(2,1)}), bf16[4,1024,512]{2,1,0:T(8,128)(2,1)}) %reduce-scatter.14.cloned.1.call-update) | async-done | bytes 4194320 | tf_op jit(solution)/shard_map/reduce_scatter | solution.py:202
  432.7 102.1 %reduce-scatter.12.cloned.1.call-done = bf16[4,256,2048]{1,2,0:T(8,128)(2,1)} async-done(((bf16[4,512,2048]{1,2,0:T(8,128)(2,1)}), bf16[4,256,2048]{1,2,0:T(8,128)(2,1)}) %reduce-scatter.12.cloned.1.call-update) | async-done | bytes 4194320 | tf_op jit(solution)/shard_map/reduce_scatter | solution.py:199
  534.8 6.2 copy.56
  543.1 4.9 all-reduce.4
  550.1 33.8 %all-reduce.2 = (bf16[256]{0:T(256)(128)(2,1)S(1)}, bf16[256]{0:T(256)(128)(2,1)S(1)}, bf16[256,4]{0,1:T(4,128)(2,1)S(1)}) all-reduce(bf16[256]{0:T(256)(128)(2,1)S(1)} %dynamic-slice.1, bf16[256]{0:T(256)(128)(2,1)S(1)} %dynamic-slice.3, bf16[256,4]{0,1:T(4,128)(2,1)S(1)} %copy.64), channel_id=1, replica_groups=mesh['rep'=16,'shard'=2] {'rep'}, use_global_device_ids=true, to_apply=%region_22.0 | all-reduce | flops 1536 | bytes 6144 | tf_op jit(solution)/shard_map/psum | solution.py:207
  585.6 91.7 %all-reduce.7.cloned.1.call-done = (bf16[256,1536]{1,0:T(8,128)(2,1)}, bf16[256,512]{1,0:T(8,128)(2,1)}, bf16[4,1024,512]{2,1,0:T(8,128)(2,1)}) async-done(((bf16[256,1536]{1,0:T(8,128)(2,1)}, bf16[256,512]{1,0:T(8,128)(2,1)}, bf16[4,1024,512]{2,1,0:T(8,128)(2,1)}), (bf16[256,1536]{1,0:T(8,128)(2,1)}, bf16[256,512]{1,0:T(8,128)(2,1)}, bf16[4,1024,512]{2,1,0:T(8,128)(2,1)})) %all-reduce.7.cloned.1.call-update) | async-done | bytes 5242896 | tf_op jit(solution)/shard_map/psum | solution.py:208
  681.5 8.8 convert_element_type.219
  690.3 315.0 %all-gather.14.cloned.1.call-done = bf16[64,256,2048]{2,1,0:T(8,128)(2,1)} async-done(((bf16[4,256,2048]{2,1,0:T(8,128)(2,1)}), bf16[64,256,2048]{2,1,0:T(8,128)(2,1)}) %all-gather.14.cloned.1.call-update) | async-done | bytes 67108880 | tf_op jit(solution)/shard_map/all_gather | solution.py:212
  1005.3 23.8 %reduce_sum.240 = bf16[4,256,2048]{2,1,0:T(8,128)(2,1)} reduce(bf16[16,4,256,2048]{3,2,1,0:T(8,128)(2,1)} %bitcast.36, bf16[]{:T(256)} %constant.88.clone.1), dimensions={0}, to_apply=%region_33.0 | reduce | flops 31457280 | bytes 71303168 | tf_op jit(solution)/shard_map/reduce_sum | solution.py:212
  1029.1 6.2 copy.65
  1035.3 6.9 copy.58
  (113 shorter events, 35.6 us)
Async XLA Ops:
  7.2 2.4 copy-start.13
  7.2 7.6 copy-start.14
  7.2 11.9 %copy-start.12 = (bf16[256,4]{0,1:T(4,128)(2,1)S(1)}, bf16[256,4]{0,1:T(4,128)(2,1)}, u32[]{:S(2)}) copy-start(bf16[256,4]{0,1:T(4,128)(2,1)} %param.15) | copy-start | bytes 6148
  7.2 16.4 %copy-start.10 = (bf16[256,512]{1,0:T(8,128)(2,1)S(1)}, bf16[256,512]{1,0:T(8,128)(2,1)}, u32[]{:S(2)}) copy-start(bf16[256,512]{1,0:T(8,128)(2,1)} %param.13) | copy-start | bytes 786436
  7.2 30.5 %copy-start.8 = (bf16[1,197,512]{2,1,0:T(8,128)(2,1)S(1)}, bf16[1,197,512]{2,1,0:T(8,128)(2,1)}, u32[]{:S(2)}) copy-start(bf16[1,197,512]{2,1,0:T(8,128)(2,1)} %param.19) | copy-start | bytes 605188
  7.2 38.0 %all-gather.8.cloned.1.call-start = ((), (), s32[]{:S(2)}) async-start(), calls=%async_computation.5 | async-start | bytes 2359296 | tf_op jit(solution)/shard_map/all_gather | solution.py:107
  8.0 142.8 %all-gather.10.cloned.1.call-start = ((), (), s32[]{:S(2)}) async-start(), calls=%async_computation.6 | async-start | bytes 12582912 | tf_op jit(solution)/shard_map/all_gather | solution.py:111
  8.7 247.7 %all-gather.12.cloned.1.call-start = ((), (), s32[]{:S(2)}) async-start(), calls=%async_computation.7 | async-start | bytes 12582912 | tf_op jit(solution)/shard_map/all_gather | solution.py:112
  9.5 300.6 %reduce-scatter.10.cloned.1.call-start = ((), (), s32[]{:S(2)}) async-start(), calls=%async_computation.9 | async-start | bytes 786432 | tf_op jit(solution)/shard_map/reduce_scatter | solution.py:190
  23.7 27.7 %copy-start.11 = (s32[1,197,2]{1,2,0:T(2,128)S(1)}, s32[1,197,2]{1,2,0:T(2,128)}, u32[]{:S(2)}) copy-start(s32[1,197,2]{1,2,0:T(2,128)} %param.18) | copy-start | bytes 4732
  51.5 204.9 %copy-start.6 = (f32[197,512]{1,0:T(8,128)S(1)}, f32[197,512]{1,0:T(8,128)}, u32[]{:S(2)}) copy-start(f32[197,512]{1,0:T(8,128)} %bitcast_convert_fusion) | copy-start | bytes 1210372
  274.2 7.5 copy-start.1
  274.2 8.1 copy-start.9
  274.2 8.9 copy-start.2
  274.2 9.9 copy-start.4
  287.0 43.6 %reduce-scatter.8.cloned.1.call-start = ((), (), s32[]{:S(2)}) async-start(), calls=%async_computation.8 | async-start | bytes 2359296 | tf_op jit(solution)/shard_map/reduce_scatter | solution.py:187
  287.3 2.7 copy-start.5
  292.5 140.1 %reduce-scatter.14.cloned.1.call-start = ((), (), s32[]{:S(2)}) async-start(), calls=%async_computation.11 | async-start | bytes 12582912 | tf_op jit(solution)/shard_map/reduce_scatter | solution.py:202
  300.5 234.3 %reduce-scatter.12.cloned.1.call-start = ((), (), s32[]{:S(2)}) async-start(), calls=%async_computation.10 | async-start | bytes 12582912 | tf_op jit(solution)/shard_map/reduce_scatter | solution.py:199
  308.6 240.5 %reduce-scatter.16.cloned.1.call-start = ((), (), s32[]{:S(2)}) async-start(), calls=%async_computation.13 | async-start | bytes 196608
  310.0 367.3 %all-reduce.7.cloned.1.call-start = ((), (), s32[]{:S(2)}) async-start(), calls=%async_computation.14 | async-start | bytes 10485760 | tf_op jit(solution)/shard_map/psum | solution.py:208
  432.6 108.4 %copy-start.15 = (u32[32]{0:T(128)S(1)}, u32[32]{0:T(128)}, u32[]{:S(2)}) copy-start(u32[32]{0:T(128)} %constant.94) | copy-start | bytes 388
  432.6 109.7 %copy-start.7 = (bf16[512,1536]{1,0:T(8,128)(2,1)S(1)}, bf16[512,1536]{1,0:T(8,128)(2,1)}, u32[]{:S(2)}) copy-start(bf16[512,1536]{1,0:T(8,128)(2,1)} %all-gather.8.cloned.1.call-done) | copy-start | bytes 4718596
  432.6 572.7 %all-gather.14.cloned.1.call-start = ((), (), s32[]{:S(2)}) async-start(), calls=%async_computation.12 | async-start | bytes 71303168 | tf_op jit(solution)/shard_map/all_gather | solution.py:212
  (2 other events, 3.0 us)
Sparse Core Ops, SparseCore 0:
  9.6 35.5 all-gather.7
  46.7 103.9 all-gather.9
  152.3 103.9 all-gather.11
  287.1 14.5 reduce-scatter.9
  304.5 26.0 reduce-scatter.7
  333.3 99.2 reduce-scatter.13
  435.6 99.2 reduce-scatter.11
  537.0 10.2 reduce-scatter.15
  551.4 125.7 all-reduce.6
  679.3 325.9 all-gather.13
